TPU v7x, 32 devices: a whole 2x2x4 slice. The times are simulated.
32 devices in a mesh: shard: 2 (over y), blk: 4 (over z), ckpt: 2 (over x), qry: 2 (over core).
Axes of the slice: x: 2, y: 2, z: 4, core: 2. Of those that a mesh axis runs over, the one named last changes fastest.
Arguments:
- query_feats: bfloat16 [2, 8192, 2048], P('ckpt', ('shard', 'blk', 'qry')), parts along dimension 1, may hold values from -6 to 6
- train_feats: bfloat16 [2, 1024, 2048], P('ckpt', ('shard', 'blk')), parts along dimension 1, may hold values from -0.125 to 0.125
- loss_weights: bfloat16 [2, 1024], P('ckpt', ('shard', 'blk')), parts along dimension 1, may hold values from 0.099609375 to 1
- pair_list: int32 [32, 2], P(('shard', 'blk', 'qry')), parts along dimension 0, may hold values from 0 to 3, all different within a row
- tile_owner: int32 [8], P('shard'), parts along dimension 0, may hold values from 0 to 3, each once
Outputs:
- scores: float32 [8192, 512], P(('shard', 'blk', 'qry'), 'ckpt'), parts along dimension 0
There are 2 independent parts, one for each index of `shard`. A program takes and returns all parts, laid end to end along the dimension named above; each array names one. Nothing has to cross between parts.
Inputs may be any that keep to these rules, and one draw needn't show every extreme that they name: `pair_list`: each row names 2 different training blocks; every training block is named by some row. `tile_owner`: a permutation of the training blocks.
All inputs are finite; a program needn't handle non-finite values.
Results may differ from a plain program's by a relative error of at most 0.0003.
Values may be sent and summed in bfloat16 or wider, within the bound.
No kernel may reach another device: no remote copies, remote signals or barrier semaphores. Data moves between devices by JAX's collectives and lax.ppermute only.
A program may use at most 128 MiB of HBM per device.

v0:
```python
import jax
import jax.numpy as jnp
from jax import lax
from jax.sharding import PartitionSpec as P

QBLK = 256
TBLK = 128


def per_device(query_feats, train_feats, loss_weights, pair_list, tile_owner):
    queries = query_feats[0]
    block_count = lax.axis_size("blk")
    total_rows = TBLK * block_count
    block_ids = jnp.arange(block_count, dtype=jnp.int32)
    wanted = jnp.any(pair_list[:, :, None] == block_ids[None, None, :], axis=1).astype(jnp.float32)
    own_rows = train_feats[0]
    own_weights = loss_weights[0]
    gathered_rows, gathered_weights = (
        lax.all_gather(own_rows, "blk", axis=0, tiled=True),
        lax.all_gather(own_weights, "blk", axis=0, tiled=True),
    )
    row_blocks = gathered_rows.reshape(block_count, TBLK, gathered_rows.shape[1])
    weight_blocks = gathered_weights.reshape(block_count, TBLK)
    query_mask = jnp.transpose(jnp.repeat(wanted, QBLK, axis=0))
    owner_rows = total_rows // lax.axis_size("ckpt")
    picked = row_blocks[tile_owner].reshape(lax.axis_size("ckpt") * owner_rows, row_blocks.shape[2])
    picked_weights = (
        weight_blocks[tile_owner].reshape(lax.axis_size("ckpt") * owner_rows).astype(jnp.float32)
    )
    products = lax.dot_general(
        picked, queries, (((1,), (1,)), ((), ())), preferred_element_type=jnp.float32
    )
    mask_rows = jnp.repeat(query_mask[tile_owner], TBLK, axis=0)
    summed_rows = lax.psum_scatter(
        products * picked_weights[:, None] * mask_rows, "ckpt", scatter_dimension=0, tiled=True
    )
    return jnp.transpose(summed_rows)


def solution(mesh):
    return jax.shard_map(
        per_device,
        mesh=mesh,
        in_specs=(
            P("ckpt", ("shard", "blk", "qry"), None),
            P("ckpt", ("shard", "blk"), None),
            P("ckpt", ("shard", "blk")),
            P(("shard", "blk", "qry"), None),
            P("shard"),
        ),
        out_specs=P(("shard", "blk", "qry"), "ckpt"),
        check_vma=False,
    )
```

profile of v0, /device:TPU:0, one launch (start us, length us, event | category | flops | bytes accessed | tf_op | source)
XLA Modules:
  0.0 93.2 jit_solution(14550216381288683997)
XLA Ops:
  6.5 0.0 copy-start
  6.5 0.0 all-gather.4.cloned.1.call-start
  6.5 0.7 all-gather.4.cloned.1.call-update
  7.3 0.0 reduce-scatter.2.cloned.1.call-start
  7.3 0.8 compare_reduce_fusion
  8.1 0.1 copy.7
  8.2 0.1 broadcast_bitcast_fusion
  8.3 0.7 compare_select_fusion
  8.9 0.6 gather_fusion.2
  9.5 12.8 %all-gather.1 = bf16[1,512]{1,0:T(2,128)(2,1)S(1)} all-gather(bf16[1,128]{1,0:T(2,128)(2,1)} %param.7), channel_id=3, replica_groups=mesh['shard'=2,'blk'=4,'ckpt'=2,'qry'=2] {'blk'}, dimensions={1}, use_global_device_ids=true | all-gather | bytes 1280 | tf_op jit(solution)/shard_map/all_gather | solution.py:20
  22.3 0.6 gather_fusion.1
  22.9 34.4 %all-gather.4.cloned.1.call-done = bf16[1,512,2048]{2,1,0:T(8,128)(2,1)} async-done(((bf16[1,128,2048]{2,1,0:T(8,128)(2,1)}), bf16[1,512,2048]{2,1,0:T(8,128)(2,1)}) %all-gather.4.cloned.1.call-update) | async-done | bytes 2097168 | tf_op jit(solution)/shard_map/all_gather | solution.py:19
  57.3 3.6 %gather_fusion = bf16[4,128,2048]{2,1,0:T(8,128)(2,1)} fusion(bf16[4,128,2048]{2,1,0:T(8,128)(2,1)} %bitcast.23, s32[1024]{0:T(1024)S(1)} %pad_clamp_fusion), kind=kCustom, calls=%fused_computation | custom fusion | bytes 4194320 | tf_op jit(solution)/shard_map/gather | solution.py:26
  60.9 0.1 broadcast_in_dim.16
  61.1 0.0 copy-done
  61.1 3.9 %fusion.5 = f32[512,512]{1,0:T(8,128)} fusion(f32[512,512]{1,0:T(8,128)S(1)} %bitcast.25, bf16[512,2048]{1,0:T(8,128)(2,1)} %bitcast.24, bf16[1,512,2048]{2,1,0:T(8,128)(2,1)S(1)} %copy-done, f32[512]{0:T(512)S(1)} %bitcast_convert_fusion), kind=kOutput, calls=%fused_computation.6 | convolution fusion | flops 1074266112 | bytes 6293504 | tf_op jit(solution)/shard_map/dot_general | solution.py:30
  64.9 0.0 reduce-scatter.2.cloned.1.call-update
  65.0 19.3 %reduce-scatter.2.cloned.1.call-done = f32[256,512]{1,0:T(8,128)} async-done(((f32[512,512]{1,0:T(8,128)}), f32[256,512]{1,0:T(8,128)}) %reduce-scatter.2.cloned.1.call-update) | async-done | bytes 524304 | tf_op jit(solution)/shard_map/reduce_scatter | solution.py:34
  84.3 2.0 %copy.8 = f32[512,256]{1,0:T(8,128)} copy(f32[512,256]{0,1:T(8,128)} %bitcast.27) | data formatting | bytes 1048576 | tf_op jit(solution)/shard_map/transpose | solution.py:37
  (5 shorter events, 0.0 us)
Async XLA Ops:
  6.5 54.5 %copy-start = (bf16[1,512,2048]{2,1,0:T(8,128)(2,1)S(1)}, bf16[1,512,2048]{2,1,0:T(8,128)(2,1)}, u32[]{:S(2)}) copy-start(bf16[1,512,2048]{2,1,0:T(8,128)(2,1)} %param.5) | copy-start | bytes 6291460
  6.5 50.8 %all-gather.4.cloned.1.call-start = ((), (), s32[]{:S(2)}) async-start(), calls=%async_computation.2 | async-start | bytes 2621440 | tf_op jit(solution)/shard_map/all_gather | solution.py:19
  7.3 77.0 %reduce-scatter.2.cloned.1.call-start = ((), (), s32[]{:S(2)}) async-start(), calls=%async_computation.1 | async-start | bytes 1572864 | tf_op jit(solution)/shard_map/reduce_scatter | solution.py:34
Sparse Core Ops, SparseCore 0:
  8.9 48.3 all-gather.3
  65.1 19.1 reduce-scatter.1
where the time goes:
time: 93.4 us; the launch traced here: 93.2 us
  waiting for transfers between devices  54.5 us (58%)
  between operations  13.4 us (14%)
  blocking collectives  12.8 us (14%)
  local copies, waits for them, and re-layouts  7.07 us (8%)
  matrix products  3.86 us (4%)
  other arithmetic  1.47 us (2%)
    all_gather x1, waiting for transfers between devices, per_device(): lax.all_gather(own_rows, 'blk', axis=0, tiled=True)  34.4 us
    reduce_scatter x1, waiting for transfers between devices, per_device(): lax.psum_scatter(products * picked_weights[:, None] * mask_rows, 'ckpt',...  19.3 us
    all_gather x1, blocking collectives, per_device(): lax.all_gather(own_weights, 'blk', axis=0, tiled=True)  12.8 us
    dot_general x1, matrix products, per_device(): lax.dot_general(picked, queries, (((1,), (1,)), ((), ())), preferred_elem...  3.86 us
    gather x1, local copies, waits for them, and re-layouts, per_device(): row_blocks[tile_owner]  3.62 us
    transpose x1, local copies, waits for them, and re-layouts, per_device(): return jnp.transpose(summed_rows)  2.04 us
  transfers between devices with their start and end apart: 2, of which 2 were waited for; matrix products, arithmetic and copies ran while one was open for 3% of the time, Pallas kernels for 0%

commit v1 on v0

--- a/solution.py
+++ b/solution.py
@@ -5,6 +5,27 @@
 
 QBLK = 256
 TBLK = 128
+
+
+def laid_out(pieces, dim):
+    lengths = list(pieces.shape[1:])
+    lengths[dim] *= pieces.shape[0]
+    return jnp.moveaxis(pieces, 0, dim).reshape(lengths)
+
+
+def collected_by_bits(value, axis):
+    size, index = (lax.axis_size(axis), lax.axis_index(axis))
+    parts, stride = (value[None], 1)
+    while stride < size:
+        received = lax.ppermute(parts, axis, [(i, i ^ stride) for i in range(size)])
+        low = index & stride == 0
+        parts = jnp.concatenate([jnp.where(low, parts, received), jnp.where(low, received, parts)])
+        stride *= 2
+    return parts
+
+
+def collect(shard, axis, dim):
+    return laid_out(collected_by_bits(shard, axis), dim)
 
 
 def per_device(query_feats, train_feats, loss_weights, pair_list, tile_owner):
@@ -16,7 +37,7 @@
     own_rows = train_feats[0]
     own_weights = loss_weights[0]
     gathered_rows, gathered_weights = (
-        lax.all_gather(own_rows, "blk", axis=0, tiled=True),
+        collect(own_rows, "blk", 0),
         lax.all_gather(own_weights, "blk", axis=0, tiled=True),
     )
     row_blocks = gathered_rows.reshape(block_count, TBLK, gathered_rows.shape[1])

time: 93.4 us -> 116 us (1.24)
  blocking collectives: 12.8 us -> 26.8 us
  starting transfers between devices: 0.04 us -> 5.81 us
  other arithmetic: 1.47 us -> 5.32 us
    all_gather x1 -> x0, waiting for transfers between devices: 34.4 us -> none  [per_device(): lax.all_gather(own_rows, 'blk', axis=0, tiled=True)]
    ppermute x0 -> x2, waiting for transfers between devices: none -> 29.2 us  [collected_by_bits(): received = lax.ppermute(parts, axis, [(i, i ^ stride) for i in range(size)])]
    all_gather x1, blocking collectives: 12.8 us -> 26.8 us  [per_device(): lax.all_gather(own_weights, 'blk', axis=0, tiled=True)]
    ppermute x0 -> x2, starting transfers between devices: none -> 5.81 us  [collected_by_bits(): received = lax.ppermute(parts, axis, [(i, i ^ stride) for i in range(size)])]
    reduce_scatter x1, waiting for transfers between devices: 19.3 us -> 24.2 us  [per_device(): lax.psum_scatter(products * picked_weights[:, None] * mask_rows, 'ckpt',...]
    select_n x0 -> x2, other arithmetic: none -> 2.64 us  [collected_by_bits(): jnp.where(low, parts, received)]
    concatenate x0 -> x2, other arithmetic: none -> 2.55 us  [collected_by_bits(): jnp.concatenate([jnp.where(low, parts, received), jnp.where(low, received...]
  transfers between devices with their start and end apart: 2 -> 3, of which waited for: 2 -> 3; matrix products, arithmetic and copies ran while one was open for 3% -> 1% of each run, Pallas kernels for 0% -> 0%
where the time goes in v1:
time: 116 us
  waiting for transfers between devices  53.4 us (46%)
  blocking collectives  26.8 us (23%)
  between operations  13.4 us (12%)
  local copies, waits for them, and re-layouts  7.07 us (6%)
  starting transfers between devices  5.81 us (5%)
  other arithmetic  5.32 us (5%)
  matrix products  3.88 us (3%)
    ppermute x2, waiting for transfers between devices, collected_by_bits(): received = lax.ppermute(parts, axis, [(i, i ^ stride) for i in range(size)])  29.2 us
    all_gather x1, blocking collectives, per_device(): lax.all_gather(own_weights, 'blk', axis=0, tiled=True)  26.8 us
    reduce_scatter x1, waiting for transfers between devices, per_device(): lax.psum_scatter(products * picked_weights[:, None] * mask_rows, 'ckpt',...  24.2 us
    ppermute x2, starting transfers between devices, collected_by_bits(): received = lax.ppermute(parts, axis, [(i, i ^ stride) for i in range(size)])  5.81 us
    dot_general x1, matrix products, per_device(): lax.dot_general(picked, queries, (((1,), (1,)), ((), ())), preferred_elem...  3.88 us
    gather x1, local copies, waits for them, and re-layouts, per_device(): row_blocks[tile_owner]  3.61 us
    select_n x2, other arithmetic, collected_by_bits(): jnp.where(low, parts, received)  2.64 us
    concatenate x2, other arithmetic, collected_by_bits(): jnp.concatenate([jnp.where(low, parts, received), jnp.where(low, received...  2.55 us
  transfers between devices with their start and end apart: 3, of which 3 were waited for; matrix products, arithmetic and copies ran while one was open for 1% of the time, Pallas kernels for 0%

profile of v1, /device:TPU:0, one launch (start us, length us, event | category | flops | bytes accessed | tf_op | source)
XLA Modules:
  0.0 115.8 jit_solution(1013740103934778733)
XLA Ops:
  6.5 0.0 copy-start
  6.5 0.0 reduce-scatter.2.cloned.1.call-start
  6.5 3.1 %collective-permute-start = (bf16[1,128,2048]{2,1,0:T(8,128)(2,1)}, bf16[1,128,2048]{2,1,0:T(8,128)(2,1)}, u32[]{:S(2)}, u32[]{:S(2)}) collective-permute-start(bf16[1,128,2048]{2,1,0:T(8,128)(2,1)} %param.6), channel_id=1, source_target_pairs={{0,4},{4,0},{8,12},{12,8},{1,5},{5,1},{9,13},{13,9},{2,6},{6,2},{1... | collective-permute-start | bytes 1572872 | tf_op jit(solution)/shard_map/ppermute | solution.py:20
  9.6 0.0 copy-start.2
  9.6 0.0 copy-start.3
  9.6 0.0 copy-start.1
  9.6 12.2 %collective-permute-done = bf16[1,128,2048]{2,1,0:T(8,128)(2,1)} collective-permute-done((bf16[1,128,2048]{2,1,0:T(8,128)(2,1)}, bf16[1,128,2048]{2,1,0:T(8,128)(2,1)}, u32[]{:S(2)}, u32[]{:S(2)}) %collective-permute-start) | collective-permute-done | bytes 524320 | tf_op jit(solution)/shard_map/ppermute | solution.py:20
  21.8 1.3 %broadcast_select_fusion.3 = (bf16[1,128,2048]{2,1,0:T(8,128)(2,1)S(1)}, bf16[1,128,2048]{2,1,0:T(8,128)(2,1)S(1)}) fusion(bf16[1,128,2048]{2,1,0:T(8,128)(2,1)} %param.6, bf16[1,128,2048]{2,1,0:T(8,128)(2,1)} %collective-permute-done, pred[]{:T(512)S(6)} %eq.20), kind=kLoop, calls=%fused_computation.12 | loop fusion | flops 524288 | bytes 2097153 | tf_op jit(solution)/shard_map/jit(_where)/select_n | solution.py:22
  23.1 1.1 pad_maximum_fusion.1
  24.2 2.8 %collective-permute-start.1 = (bf16[2,128,2048]{2,1,0:T(8,128)(2,1)}, bf16[2,128,2048]{2,1,0:T(8,128)(2,1)}, u32[]{:S(2)}, u32[]{:S(2)}) collective-permute-start(bf16[2,128,2048]{2,1,0:T(8,128)(2,1)} %pad_maximum_fusion.1), channel_id=1, source_target_pairs={{0,8},{4,12},{8,0},{12,4},{1,9},{5,13},{9,1},{13,5},{2,10},{6,14},... | collective-permute-start | bytes 3145736 | tf_op jit(solution)/shard_map/ppermute | solution.py:20
  26.9 0.0 copy-done.2
  26.9 0.1 compare_reduce_fusion
  27.0 0.1 copy.7
  27.1 0.1 broadcast_bitcast_fusion
  27.2 0.0 copy-done.3
  27.2 0.6 gather_fusion.2
  27.8 0.0 copy-done.1
  27.8 26.8 %all-gather = bf16[1,512]{1,0:T(2,128)(2,1)S(1)} all-gather(bf16[1,128]{1,0:T(2,128)(2,1)S(1)} %copy-done.1), channel_id=2, replica_groups=mesh['shard'=2,'blk'=4,'ckpt'=2,'qry'=2] {'blk'}, dimensions={1}, use_global_device_ids=true | all-gather | bytes 1280 | tf_op jit(solution)/shard_map/all_gather | solution.py:41
  54.7 0.6 gather_fusion.1
  55.2 17.0 %collective-permute-done.1 = bf16[2,128,2048]{2,1,0:T(8,128)(2,1)} collective-permute-done((bf16[2,128,2048]{2,1,0:T(8,128)(2,1)}, bf16[2,128,2048]{2,1,0:T(8,128)(2,1)}, u32[]{:S(2)}, u32[]{:S(2)}) %collective-permute-start.1) | collective-permute-done | bytes 1048608 | tf_op jit(solution)/shard_map/ppermute | solution.py:20
  72.2 1.4 %broadcast_select_fusion.1 = (bf16[2,128,2048]{2,1,0:T(8,128)(2,1)S(1)}, bf16[2,128,2048]{2,1,0:T(8,128)(2,1)S(1)}) fusion(bf16[2,128,2048]{2,1,0:T(8,128)(2,1)} %collective-permute-done.1, pred[]{:T(512)S(6)} %eq.19, bf16[1,128,2048]{2,1,0:T(8,128)(2,1)S(1)} %get-tuple-element.8, bf16[1,128,2048]{2,1,0:T(8,128)(2,1)S(1)} %get-tuple-element.7), kind=kLoop, calls=%fused_computation.10 | loop fusion | flops 1572864 | bytes 4194305 | tf_op jit(solution)/shard_map/jit(_where)/select_n | solution.py:22
  73.6 1.5 %pad_maximum_fusion = bf16[4,128,2048]{2,1,0:T(8,128)(2,1)} fusion(bf16[2,128,2048]{2,1,0:T(8,128)(2,1)S(1)} %get-tuple-element.6, bf16[2,128,2048]{2,1,0:T(8,128)(2,1)S(1)} %get-tuple-element.5), kind=kLoop, calls=%fused_computation.3 | loop fusion | flops 1048576 | bytes 4194304 | tf_op jit(solution)/shard_map/concatenate | solution.py:22
  75.1 3.6 %gather_fusion = bf16[4,128,2048]{2,1,0:T(8,128)(2,1)} fusion(bf16[4,128,2048]{2,1,0:T(8,128)(2,1)} %pad_maximum_fusion, s32[1024]{0:T(1024)S(1)} %pad_clamp_fusion), kind=kCustom, calls=%fused_computation | custom fusion | bytes 4194320 | tf_op jit(solution)/shard_map/gather | solution.py:47
  78.7 0.1 broadcast_in_dim.16
  78.8 0.0 copy-done
  78.8 3.9 %fusion.5 = f32[512,512]{1,0:T(8,128)} fusion(f32[512,512]{1,0:T(8,128)S(1)} %bitcast.23, bf16[512,2048]{1,0:T(8,128)(2,1)} %bitcast.22, bf16[1,512,2048]{2,1,0:T(8,128)(2,1)S(1)} %copy-done, f32[512]{0:T(512)S(1)} %bitcast_convert_fusion), kind=kOutput, calls=%fused_computation.7 | convolution fusion | flops 1074266112 | bytes 6293504 | tf_op jit(solution)/shard_map/dot_general | solution.py:51
  82.7 0.0 reduce-scatter.2.cloned.1.call-update
  82.7 24.2 %reduce-scatter.2.cloned.1.call-done = f32[256,512]{1,0:T(8,128)} async-done(((f32[512,512]{1,0:T(8,128)}), f32[256,512]{1,0:T(8,128)}) %reduce-scatter.2.cloned.1.call-update) | async-done | bytes 524304 | tf_op jit(solution)/shard_map/reduce_scatter | solution.py:55
  106.9 2.0 %copy.8 = f32[512,256]{1,0:T(8,128)} copy(f32[512,256]{0,1:T(8,128)} %bitcast.25) | data formatting | bytes 1048576 | tf_op jit(solution)/shard_map/transpose | solution.py:58
  (6 shorter events, 0.1 us)
Async XLA Ops:
  6.5 72.3 %copy-start = (bf16[1,512,2048]{2,1,0:T(8,128)(2,1)S(1)}, bf16[1,512,2048]{2,1,0:T(8,128)(2,1)}, u32[]{:S(2)}) copy-start(bf16[1,512,2048]{2,1,0:T(8,128)(2,1)} %param.5) | copy-start | bytes 6291460
  6.5 100.3 %reduce-scatter.2.cloned.1.call-start = ((), (), s32[]{:S(2)}) async-start(), calls=%async_computation.1 | async-start | bytes 1572864 | tf_op jit(solution)/shard_map/reduce_scatter | solution.py:55
  6.5 15.3 %collective-permute-start = (bf16[1,128,2048]{2,1,0:T(8,128)(2,1)}, bf16[1,128,2048]{2,1,0:T(8,128)(2,1)}, u32[]{:S(2)}, u32[]{:S(2)}) collective-permute-start(bf16[1,128,2048]{2,1,0:T(8,128)(2,1)} %param.6), channel_id=1, source_target_pairs={{0,4},{4,0},{8,12},{12,8},{1,5},{5,1},{9,13},{13,9},{2,6},{6,2},{1... | collective-permute-start | bytes 1572872 | tf_op jit(solution)/shard_map/ppermute | solution.py:20
  9.6 17.3 %copy-start.2 = (s32[2,2]{1,0:T(2,128)S(1)}, s32[2,2]{1,0:T(2,128)}, u32[]{:S(2)}) copy-start(s32[2,2]{1,0:T(2,128)} %param.8) | copy-start | bytes 52
  9.6 17.6 %copy-start.3 = (s32[4]{0:T(128)S(1)}, s32[4]{0:T(128)}, u32[]{:S(2)}) copy-start(s32[4]{0:T(128)} %param.9) | copy-start | bytes 52
  9.6 18.2 %copy-start.1 = (bf16[1,128]{1,0:T(2,128)(2,1)S(1)}, bf16[1,128]{1,0:T(2,128)(2,1)}, u32[]{:S(2)}) copy-start(bf16[1,128]{1,0:T(2,128)(2,1)} %param.7) | copy-start | bytes 772
  24.2 48.0 %collective-permute-start.1 = (bf16[2,128,2048]{2,1,0:T(8,128)(2,1)}, bf16[2,128,2048]{2,1,0:T(8,128)(2,1)}, u32[]{:S(2)}, u32[]{:S(2)}) collective-permute-start(bf16[2,128,2048]{2,1,0:T(8,128)(2,1)} %pad_maximum_fusion.1), channel_id=1, source_target_pairs={{0,8},{4,12},{8,0},{12,4},{1,9},{5,13},{9,1},{13,5},{2,10},{6,14},... | collective-permute-start | bytes 3145736 | tf_op jit(solution)/shard_map/ppermute | solution.py:20
Sparse Core Ops, SparseCore 0:
  82.8 24.0 reduce-scatter.1
